TPU v7x, 256 devices: a whole 4x4x8 slice. The times are simulated.
256 devices in a mesh: rows: 8 (over z), cols: 32 (over y, x, core).
Axes of the slice: x: 4, y: 4, z: 8, core: 2. Of those that a mesh axis runs over, the one named last changes fastest.
Arguments:
- whitened: float32 [3, 1048576], P(None, ('rows', 'cols')), may hold values from -6 to 6
- cotangent: bfloat16 [64, 1048576], P(None, ('rows', 'cols')), may hold values from -6 to 6
- lift_weight: float32 [64, 3], replicated, may hold values from -3.5 to 3.5
- conv_now: bfloat16 [3, 128, 64], replicated, may hold values from -0.5 to 0.5
- conv_past: bfloat16 [3, 128, 64], replicated, may hold values from -0.5 to 0.5
- mix_weight: bfloat16 [3, 64, 64], replicated, may hold values from -0.75 to 0.75
- dilations: int32 [3], replicated, may hold values from 64 to 256, as said below
- psd_bin: int32 [4096, 32, 8], P(None, 'cols', 'rows'), may hold values from 0 to 1023, as said below
- psd_weight: float32 [2, 1024], replicated, may hold values from 0.2 to 5
Outputs:
- data_grad: float32 [3, 1048576], P(None, ('rows', 'cols'))
- grad_now: float32 [3, 128, 64], replicated
- grad_past: float32 [3, 128, 64], replicated
- grad_mix: float32 [3, 64, 64], replicated
- grad_lift: float32 [64, 3], replicated
Inputs may be any that keep to these rules, and one draw needn't show every extreme that they name: `dilations`: multiples of 4; one layer has 64, one has 256. `psd_bin`: frequencies k and 1048576 - k have the same bin.
All inputs are finite; a program needn't handle non-finite values.
Results may differ from a plain program's by a relative error of at most 0.0068.
Values may be sent and summed in bfloat16 or wider, within the bound.
No kernel may reach another device: no remote copies, remote signals or barrier semaphores. Data moves between devices by JAX's collectives and lax.ppermute only.
A program may use at most 64 MiB of HBM per device.

v0:
```python
import math
import jax
import jax.numpy as jnp
from jax import lax
from jax.sharding import PartitionSpec as P

DMAX = 256


def from_behind(array, axis, by):
    peers = lax.axis_size(axis)
    pairs = [(i, i + by) for i in range(peers) if 0 <= i + by < peers]
    return lax.ppermute(array, axis, pairs)


def lifted(lift_weight, inputs):
    return (
        lift_weight[:, 0:1] * inputs[0:1]
        + lift_weight[:, 1:2] * inputs[1:2]
        + lift_weight[:, 2:3] * inputs[2:3]
    )


def delayed(field_b, delay, before):
    joined = jnp.concatenate([before, field_b], axis=1)
    start_at = before.shape[1] - delay
    return lax.dynamic_slice_in_dim(joined, start_at, field_b.shape[1], 1)


def advanced(values, delay, head_rim):
    joined = jnp.concatenate([values, head_rim], axis=1)
    return lax.dynamic_slice_in_dim(joined, delay, values.shape[1], 1)


def gated_layer(field_now, field_b, before, weight_now, weight_past, weight_mix, delay):
    channel_count = weight_mix.shape[0]
    past_b = delayed(field_b, delay, before)
    pre_act = jnp.dot(weight_now, field_b, preferred_element_type=jnp.float32) + jnp.dot(
        weight_past, past_b, preferred_element_type=jnp.float32
    )
    tanh_part = jnp.tanh(pre_act[:channel_count])
    sigm_part = jax.nn.sigmoid(pre_act[channel_count:])
    gate_b = (tanh_part * sigm_part).astype(jnp.bfloat16)
    field_next = field_now + jnp.dot(weight_mix, gate_b, preferred_element_type=jnp.float32)
    return (field_next, (field_b, past_b, tanh_part, sigm_part, gate_b))


def phase_angle(product, modulus, sign_factor):
    return sign_factor * 2.0 * math.pi / modulus * (product % modulus).astype(jnp.float32)


def phase_table(modulus, sign_factor):
    ordinal = jnp.arange(modulus, dtype=jnp.int32)
    angles = phase_angle(ordinal[:, None] * ordinal[None, :], modulus, sign_factor)
    return (jnp.cos(angles), jnp.sin(angles))


def rotate(signals, angles):
    real_part, imag_part = signals
    cosine = jnp.cos(angles)
    sine_part = jnp.sin(angles)
    return (real_part * cosine - imag_part * sine_part, real_part * sine_part + imag_part * cosine)


def transform(pattern, table_pair, signals):
    cosine, sine_part = table_pair
    real_part, imag_part = signals
    first_term = jnp.einsum(pattern, cosine, real_part, precision=lax.Precision.HIGHEST)
    second = jnp.einsum(pattern, sine_part, real_part, precision=lax.Precision.HIGHEST)
    if imag_part is None:
        return (first_term, second)
    return (
        first_term - jnp.einsum(pattern, sine_part, imag_part, precision=lax.Precision.HIGHEST),
        second + jnp.einsum(pattern, cosine, imag_part, precision=lax.Precision.HIGHEST),
    )


def split_length(length_all):
    chosen = 1
    for factor in range(1, length_all + 1):
        if length_all % factor == 0 and factor * factor <= length_all:
            chosen = factor
    return (chosen, length_all // chosen)


def pair_up(moved):
    return ((moved, None), (0, 0, 1))


def local_section(signals, psd_bin, psd_weight, weight_rows):
    rows_count = lax.axis_size("rows")
    row_index = lax.axis_index("rows")
    col_index = lax.axis_index("cols")
    signal_count = len(weight_rows)
    segment = signals[0].shape[1]
    length_all = segment * rows_count * lax.axis_size("cols")
    slow_len, fast_len = split_length(segment)
    slow_ids = jnp.arange(slow_len, dtype=jnp.int32)
    fast_ids = jnp.arange(fast_len, dtype=jnp.int32)
    spectra = (
        signals[0].reshape(signal_count, slow_len, fast_len),
        signals[1].reshape(signal_count, slow_len, fast_len),
    )
    spectra = transform("pa,kpq->kaq", phase_table(slow_len, -1.0), spectra)
    spectra = rotate(
        spectra, phase_angle(slow_ids[:, None] * fast_ids[None, :], segment, -1.0)[None]
    )
    spectra = transform("qb,kaq->kab", phase_table(fast_len, -1.0), spectra)
    bins_here = psd_bin.reshape(fast_len, slow_len).T
    weights = jnp.take(psd_weight, bins_here, axis=1)
    factors = jnp.stack([weights[row_id] for row_id in weight_rows])
    spectra = (spectra[0] * factors, spectra[1] * factors)
    spectra = transform("bq,kab->kaq", phase_table(fast_len, 1.0), spectra)
    spectra = rotate(
        spectra, phase_angle(slow_ids[:, None] * fast_ids[None, :], segment, 1.0)[None]
    )
    spectra = transform("ap,kaq->kpq", phase_table(slow_len, 1.0), spectra)
    low_here = row_index + rows_count * col_index
    sample_all = jnp.arange(segment, dtype=jnp.int32)
    return rotate(
        (spectra[0].reshape(signal_count, segment), spectra[1].reshape(signal_count, segment)),
        phase_angle(sample_all * low_here, length_all, 1.0)[None],
    )


def per_axis_filter(signal, psd_bin, psd_weight):
    rows_count = lax.axis_size("rows")
    cols_count = lax.axis_size("cols")
    row_index = lax.axis_index("rows")
    col_index = lax.axis_index("cols")
    segment = signal.shape[1]
    groups = rows_count * cols_count
    length_all = segment * groups
    piece_len = segment // rows_count
    small_len = segment // groups
    outer_ids = jnp.arange(rows_count, dtype=jnp.int32)
    inner_ids = jnp.arange(cols_count, dtype=jnp.int32)
    moved = lax.all_to_all(
        signal.reshape(3, 1, segment), "rows", split_axis=2, concat_axis=1, tiled=True
    )
    signals, weight_rows = pair_up(moved)
    signal_count = len(weight_rows)
    signals = transform("ra,krj->kaj", phase_table(rows_count, -1.0), signals)
    signals = rotate(signals, phase_angle(col_index * outer_ids, groups, -1.0)[None, :, None])
    pieces = (
        lax.all_to_all(
            signals[0].reshape(signal_count, rows_count, 1, piece_len),
            "cols",
            split_axis=3,
            concat_axis=2,
            tiled=True,
        ),
        lax.all_to_all(
            signals[1].reshape(signal_count, rows_count, 1, piece_len),
            "cols",
            split_axis=3,
            concat_axis=2,
            tiled=True,
        ),
    )
    turned = transform("cb,kacm->kabm", phase_table(cols_count, -1.0), (pieces[0], pieces[1]))
    freq_low = outer_ids[:, None, None] + rows_count * inner_ids[None, :, None]
    sample_at = (
        row_index * piece_len
        + col_index * small_len
        + jnp.arange(small_len, dtype=jnp.int32)[None, None, :]
    )
    turned = rotate(turned, phase_angle(sample_at * freq_low, length_all, -1.0)[None])
    signals = (
        lax.all_to_all(turned[0], "cols", split_axis=2, concat_axis=3, tiled=True),
        lax.all_to_all(turned[1], "cols", split_axis=2, concat_axis=3, tiled=True),
    )
    signals = (
        lax.all_to_all(
            signals[0].reshape(signal_count, rows_count, piece_len),
            "rows",
            split_axis=1,
            concat_axis=2,
            tiled=True,
        ),
        lax.all_to_all(
            signals[1].reshape(signal_count, rows_count, piece_len),
            "rows",
            split_axis=1,
            concat_axis=2,
            tiled=True,
        ),
    )
    flat = local_section(
        (signals[0].reshape(signal_count, segment), signals[1].reshape(signal_count, segment)),
        psd_bin,
        psd_weight,
        weight_rows,
    )
    returned = (
        lax.all_to_all(
            flat[0].reshape(signal_count, 1, segment),
            "rows",
            split_axis=2,
            concat_axis=1,
            tiled=True,
        ),
        lax.all_to_all(
            flat[1].reshape(signal_count, 1, segment),
            "rows",
            split_axis=2,
            concat_axis=1,
            tiled=True,
        ),
    )
    pieces = (
        lax.all_to_all(
            returned[0].reshape(signal_count, rows_count, 1, piece_len),
            "cols",
            split_axis=3,
            concat_axis=2,
            tiled=True,
        ),
        lax.all_to_all(
            returned[1].reshape(signal_count, rows_count, 1, piece_len),
            "cols",
            split_axis=3,
            concat_axis=2,
            tiled=True,
        ),
    )
    turned = transform("bc,kabm->kacm", phase_table(cols_count, 1.0), (pieces[0], pieces[1]))
    turned = rotate(
        turned, phase_angle(inner_ids[None, :, None] * outer_ids[:, None, None], groups, 1.0)[None]
    )
    returned = (
        lax.all_to_all(turned[0], "cols", split_axis=2, concat_axis=3, tiled=True),
        lax.all_to_all(turned[1], "cols", split_axis=2, concat_axis=3, tiled=True),
    )
    real_in = returned[0].reshape(signal_count, rows_count, piece_len)
    imag_in = returned[1].reshape(signal_count, rows_count, piece_len)
    cos_rows, sin_rows = phase_table(rows_count, 1.0)
    real_out = jnp.einsum(
        "ar,kaj->krj", cos_rows, real_in, precision=lax.Precision.HIGHEST
    ) - jnp.einsum("ar,kaj->krj", sin_rows, imag_in, precision=lax.Precision.HIGHEST)
    homed = lax.all_to_all(real_out, "rows", split_axis=1, concat_axis=2, tiled=True)
    return homed.reshape(3, segment) / float(length_all)


def local(
    whitened,
    cotangent,
    lift_weight,
    conv_now,
    conv_past,
    mix_weight,
    dilations,
    psd_bin,
    psd_weight,
):
    segment = whitened.shape[1]
    layer_count = mix_weight.shape[0]
    saved = []
    field_now = lifted(lift_weight, whitened)
    for layer_id in range(layer_count):
        field_b = field_now.astype(jnp.bfloat16)
        before = from_behind(field_b[:, segment - DMAX :], ("rows", "cols"), 1)
        field_now, kept_parts = gated_layer(
            field_now,
            field_b,
            before,
            conv_now[layer_id],
            conv_past[layer_id],
            mix_weight[layer_id],
            dilations[layer_id],
        )
        saved.append(kept_parts)
    grad_field = cotangent.astype(jnp.float32)
    grads_now = [None] * layer_count
    grads_past = [None] * layer_count
    grads_mix = [None] * layer_count
    for layer_id in reversed(range(layer_count)):
        field_b, past_b, tanh_part, sigm_part, gate_b = saved[layer_id]
        grad_field_b = grad_field.astype(jnp.bfloat16)
        grad_gate = jnp.dot(
            mix_weight[layer_id].T, grad_field_b, preferred_element_type=jnp.float32
        )
        grads_mix[layer_id] = jnp.dot(grad_field_b, gate_b.T, preferred_element_type=jnp.float32)
        grad_pre = jnp.concatenate(
            [
                grad_gate * sigm_part * (1.0 - tanh_part * tanh_part),
                grad_gate * tanh_part * sigm_part * (1.0 - sigm_part),
            ],
            axis=0,
        ).astype(jnp.bfloat16)
        grads_now[layer_id] = jnp.dot(grad_pre, field_b.T, preferred_element_type=jnp.float32)
        grads_past[layer_id] = jnp.dot(grad_pre, past_b.T, preferred_element_type=jnp.float32)
        ahead_term = jnp.dot(conv_past[layer_id].T, grad_pre, preferred_element_type=jnp.float32)
        head_rim = from_behind(ahead_term[:, :DMAX], ("rows", "cols"), -1)
        grad_field = (
            grad_field
            + jnp.dot(conv_now[layer_id].T, grad_pre, preferred_element_type=jnp.float32)
            + advanced(ahead_term, dilations[layer_id], head_rim)
        )
    input_grad = jnp.dot(lift_weight.T, grad_field, precision=lax.Precision.HIGHEST)
    lift_part = jnp.dot(grad_field, whitened.T, precision=lax.Precision.HIGHEST)
    summed = lax.psum(
        (jnp.stack(grads_now), jnp.stack(grads_past), jnp.stack(grads_mix), lift_part),
        ("rows", "cols"),
    )
    scaling = 1.0 / math.sqrt(float(segment * lax.axis_size("rows") * lax.axis_size("cols")))
    data_grad = per_axis_filter(input_grad, psd_bin, psd_weight)
    return (
        data_grad,
        summed[0] * scaling,
        summed[1] * scaling,
        summed[2] * scaling,
        summed[3] * scaling,
    )


def solution(mesh):
    in_specs = (
        P(None, ("rows", "cols")),
        P(None, ("rows", "cols")),
        P(),
        P(),
        P(),
        P(),
        P(),
        P(None, "cols", "rows"),
        P(),
    )
    out_specs = (P(None, ("rows", "cols")), P(), P(), P(), P())
    return jax.shard_map(local, mesh=mesh, in_specs=in_specs, out_specs=out_specs, check_vma=False)
```

profile of v0, /device:TPU:1, one launch (start us, length us, event | category | flops | bytes accessed | tf_op | source)
XLA Modules:
  0.0 555.5 jit_solution(1703089150025152943)
XLA Ops:
  9.3 4.6 collective-permute-start
  21.3 10.8 %gather_fusion = f32[4096,2]{1,0:T(8,128)S(1)} fusion(f32[2,1024]{0,1:T(8,128)S(1)} %copy.178, s32[4096]{0:T(1024)S(1)} %broadcast_clamp_fusion), kind=kCustom, calls=%fused_computation | custom fusion | bytes 81920 | tf_op jit(solution)/shard_map/jit(_take)/gather | solution.py:110
  87.3 20.4 %reduce.4 = f32[4096,3]{1,0:T(8,128)} reduce(f32[4096,1,3]{2,1,0:T(1,128)} %bitcast.335, f32[]{:T(128)} %broadcast.734), dimensions={1}, to_apply=%bitcast.265.reduce_sub_computation | reduce | bytes 98308
  111.4 21.0 %all-to-all-start = ((f32[8,1,1536]{2,1,0:T(1,128)}), f32[8,1,1536]{2,1,0:T(1,128)S(1)}, u32[]{:S(2)}, u32[]{:S(2)}) async-start(f32[8,1,1536]{2,1,0:T(1,128)} %reshape.486), calls=%async_computation | async-start | bytes 98304 | tf_op jit(solution)/shard_map/all_to_all | solution.py:138
  134.4 5.1 all-to-all-done
  140.3 4.4 reshape.487
  156.7 14.5 %all-to-all-start.1 = ((f32[32,1,384]{2,1,0:T(1,128)}), f32[32,1,384]{2,1,0:T(1,128)S(1)}, u32[]{:S(2)}, u32[]{:S(2)}) async-start(f32[32,1,384]{2,1,0:T(1,128)} %reshape.488), calls=%async_computation.1 | async-start | bytes 98304 | tf_op jit(solution)/shard_map/all_to_all | solution.py:146
  180.5 7.9 %all-to-all-start.2 = ((f32[32,1,384]{2,1,0:T(1,128)}), f32[32,1,384]{2,1,0:T(1,128)S(1)}, u32[]{:S(2)}, u32[]{:S(2)}) async-start(f32[32,1,384]{2,1,0:T(1,128)} %reshape.490), calls=%async_computation.2 | async-start | bytes 98304 | tf_op jit(solution)/shard_map/all_to_all | solution.py:153
  206.4 6.2 %all-to-all-start.3 = ((f32[32,1,384]{2,1,0:T(1,128)}), f32[32,1,384]{2,1,0:T(1,128)}, u32[]{:S(2)}, u32[]{:S(2)}) async-start(f32[32,1,384]{2,1,0:T(1,128)} %reshape.492), calls=%async_computation.3 | async-start | bytes 98304 | tf_op jit(solution)/shard_map/all_to_all | solution.py:170
  220.0 4.5 all-to-all-start.5
  242.4 4.5 all-to-all-start.6
  247.8 6.3 %all-to-all-done.6 = f32[3,8,512]{2,0,1:T(4,128)S(1)} async-done(((f32[3,8,512]{2,0,1:T(4,128)}), f32[3,8,512]{2,0,1:T(4,128)S(1)}, u32[]{:S(2)}, u32[]{:S(2)}) %all-to-all-start.6) | async-done | bytes 49184 | tf_op jit(solution)/shard_map/all_to_all | solution.py:181
  262.5 19.4 %reduce.12 = f32[4096,3]{1,0:T(8,128)} reduce(f32[4096,1,3]{2,1,0:T(1,128)S(1)} %bitcast.337, f32[]{:T(128)} %broadcast.734), dimensions={1}, to_apply=%bitcast.275.reduce_sub_computation | reduce | bytes 98308
  292.4 19.4 %reduce.16 = f32[4096,3]{1,0:T(8,128)} reduce(f32[4096,1,3]{2,1,0:T(1,128)S(1)} %bitcast.338, f32[]{:T(128)} %broadcast.734), dimensions={1}, to_apply=%bitcast.279.reduce_sub_computation | reduce | bytes 98308
  315.5 6.8 %all-to-all-start.9 = ((f32[8,1,1536]{2,1,0:T(1,128)}), f32[8,1,1536]{2,1,0:T(1,128)S(1)}, u32[]{:S(2)}, u32[]{:S(2)}) async-start(f32[8,1,1536]{2,1,0:T(1,128)} %reshape.500), calls=%async_computation.9 | async-start | bytes 98304 | tf_op jit(solution)/shard_map/all_to_all | solution.py:203
  326.2 4.3 copy.190
  335.7 6.2 %all-to-all-start.8 = ((f32[32,1,384]{2,1,0:T(1,128)}), f32[32,1,384]{2,1,0:T(1,128)S(1)}, u32[]{:S(2)}, u32[]{:S(2)}) async-start(f32[32,1,384]{2,1,0:T(1,128)} %reshape.498), calls=%async_computation.8 | async-start | bytes 98304 | tf_op jit(solution)/shard_map/all_to_all | solution.py:212
  342.8 79.2 %all-reduce = (f32[3,64,64]{2,1,0:T(8,128)S(1)}, f32[64,3]{0,1:T(4,128)S(1)}) all-reduce(f32[3,64,64]{2,1,0:T(8,128)S(1)} %pad_maximum_fusion.6, f32[64,3]{0,1:T(4,128)S(1)} %fusion.359), channel_id=1, replica_groups=mesh['rows'=8,'cols'=32] {'rows','cols'}, use_global_device_ids=true, to_apply=%region_2.0 | all-reduce | flops 12480 | bytes 99840 | tf_op jit(solution)/shard_map/psum | solution.py:302
  434.2 4.7 all-to-all-start.10
  451.9 4.8 all-to-all-start.12
  458.4 5.6 %all-to-all-done.12 = f32[32,1,384]{2,1,0:T(1,128)S(1)} async-done(((f32[32,1,384]{2,1,0:T(1,128)}), f32[32,1,384]{2,1,0:T(1,128)S(1)}, u32[]{:S(2)}, u32[]{:S(2)}) %all-to-all-start.12) | async-done | bytes 49184 | tf_op jit(solution)/shard_map/all_to_all | solution.py:233
  469.7 5.6 %all-to-all-done.11 = f32[32,1,384]{2,1,0:T(1,128)S(1)} async-done(((f32[32,1,384]{2,1,0:T(1,128)}), f32[32,1,384]{2,1,0:T(1,128)S(1)}, u32[]{:S(2)}, u32[]{:S(2)}) %all-to-all-start.11) | async-done | bytes 49184 | tf_op jit(solution)/shard_map/all_to_all | solution.py:232
  477.7 5.1 all-to-all-start.13
  482.8 63.4 %all-reduce.4.cloned.1.call-done = (f32[3,128,64]{1,2,0:T(8,128)}, f32[3,128,64]{1,2,0:T(8,128)}) async-done(((f32[3,128,64]{1,2,0:T(8,128)}, f32[3,128,64]{1,2,0:T(8,128)}), (f32[3,128,64]{1,2,0:T(8,128)}, f32[3,128,64]{1,2,0:T(8,128)})) %all-reduce.4.cloned.1.call-update) | async-done | bytes 196624 | tf_op jit(solution)/shard_map/psum | solution.py:302
  (291 shorter events, 195.4 us)
Async XLA Ops:
  8.0 24.8 %copy-start.40 = (f32[64]{0:T(128)}, f32[64]{0:T(128)S(1)}, u32[]{:S(2)}) copy-start(f32[64]{0:T(128)S(1)} %get-tuple-element.30) | copy-start | bytes 772
  9.2 37.5 %copy-start.5 = (bf16[64,4096]{1,0:T(8,128)(2,1)}, bf16[64,4096]{1,0:T(8,128)(2,1)S(1)}, u32[]{:S(2)}) copy-start(bf16[64,4096]{1,0:T(8,128)(2,1)S(1)} %fusion.33) | copy-start | bytes 1572868
  9.3 37.5 %collective-permute-start = (bf16[64,256]{1,0:T(8,128)(2,1)S(1)}, bf16[64,256]{1,0:T(8,128)(2,1)S(1)}, u32[]{:S(2)}, u32[]{:S(2)}) collective-permute-start(bf16[64,256]{1,0:T(8,128)(2,1)S(1)} %slice.140), channel_id=1, source_target_pairs={{0,1},{1,2},{2,3},{3,4},{4,5},{5,6},{6,7},{7,8},{8,9},{9,10},{10,1... | collective-permute-start | bytes 98312 | tf_op jit(solution)/shard_map/ppermute | solution.py:13
  48.5 29.5 %copy-start = (bf16[64,4096]{1,0:T(8,128)(2,1)}, bf16[64,4096]{1,0:T(8,128)(2,1)S(1)}, u32[]{:S(2)}) copy-start(bf16[64,4096]{1,0:T(8,128)(2,1)S(1)} %get-tuple-element.34) | copy-start | bytes 1572868
  48.6 3.1 collective-permute-start.1
  53.0 5.1 collective-permute-start.2
  60.9 6.2 %collective-permute-start.3 = (f32[64,256]{1,0:T(8,128)S(1)}, f32[64,256]{1,0:T(8,128)S(1)}, u32[]{:S(2)}, u32[]{:S(2)}) collective-permute-start(f32[64,256]{1,0:T(8,128)S(1)} %slice.149), channel_id=1, source_target_pairs={{1,0},{2,1},{3,2},{4,3},{5,4},{6,5},{7,6},{8,7},{9,8},{10,9},{11,1... | collective-permute-start | bytes 196616 | tf_op jit(solution)/shard_map/ppermute | solution.py:13
  68.8 5.6 %collective-permute-start.4 = (f32[64,256]{1,0:T(8,128)S(1)}, f32[64,256]{1,0:T(8,128)S(1)}, u32[]{:S(2)}, u32[]{:S(2)}) collective-permute-start(f32[64,256]{1,0:T(8,128)S(1)} %slice.150), channel_id=1, source_target_pairs={{1,0},{2,1},{3,2},{4,3},{5,4},{6,5},{7,6},{8,7},{9,8},{10,9},{11,1... | collective-permute-start | bytes 196616 | tf_op jit(solution)/shard_map/ppermute | solution.py:13
  76.1 5.6 %collective-permute-start.5 = (f32[64,256]{1,0:T(8,128)S(1)}, f32[64,256]{1,0:T(8,128)S(1)}, u32[]{:S(2)}, u32[]{:S(2)}) collective-permute-start(f32[64,256]{1,0:T(8,128)S(1)} %slice.151), channel_id=1, source_target_pairs={{1,0},{2,1},{3,2},{4,3},{5,4},{6,5},{7,6},{8,7},{9,8},{10,9},{11,1... | collective-permute-start | bytes 196616 | tf_op jit(solution)/shard_map/ppermute | solution.py:13
  111.4 28.1 %all-to-all-start = ((f32[8,1,1536]{2,1,0:T(1,128)}), f32[8,1,1536]{2,1,0:T(1,128)S(1)}, u32[]{:S(2)}, u32[]{:S(2)}) async-start(f32[8,1,1536]{2,1,0:T(1,128)} %reshape.486), calls=%async_computation | async-start | bytes 98304 | tf_op jit(solution)/shard_map/all_to_all | solution.py:138
  156.7 23.8 %all-to-all-start.1 = ((f32[32,1,384]{2,1,0:T(1,128)}), f32[32,1,384]{2,1,0:T(1,128)S(1)}, u32[]{:S(2)}, u32[]{:S(2)}) async-start(f32[32,1,384]{2,1,0:T(1,128)} %reshape.488), calls=%async_computation.1 | async-start | bytes 98304 | tf_op jit(solution)/shard_map/all_to_all | solution.py:146
  180.5 15.1 %all-to-all-start.2 = ((f32[32,1,384]{2,1,0:T(1,128)}), f32[32,1,384]{2,1,0:T(1,128)S(1)}, u32[]{:S(2)}, u32[]{:S(2)}) async-start(f32[32,1,384]{2,1,0:T(1,128)} %reshape.490), calls=%async_computation.2 | async-start | bytes 98304 | tf_op jit(solution)/shard_map/all_to_all | solution.py:153
  206.4 13.6 %all-to-all-start.3 = ((f32[32,1,384]{2,1,0:T(1,128)}), f32[32,1,384]{2,1,0:T(1,128)}, u32[]{:S(2)}, u32[]{:S(2)}) async-start(f32[32,1,384]{2,1,0:T(1,128)} %reshape.492), calls=%async_computation.3 | async-start | bytes 98304 | tf_op jit(solution)/shard_map/all_to_all | solution.py:170
  220.0 12.0 %all-to-all-start.5 = ((f32[32,1,384]{2,1,0:T(1,128)}), f32[32,1,384]{2,1,0:T(1,128)}, u32[]{:S(2)}, u32[]{:S(2)}) async-start(f32[32,1,384]{2,1,0:T(1,128)} %reshape.494), calls=%async_computation.5 | async-start | bytes 98304 | tf_op jit(solution)/shard_map/all_to_all | solution.py:171
  232.0 10.4 %all-to-all-start.4 = ((f32[3,8,512]{2,0,1:T(4,128)}), f32[3,8,512]{2,0,1:T(4,128)S(1)}, u32[]{:S(2)}, u32[]{:S(2)}) async-start(f32[3,8,512]{2,0,1:T(4,128)} %reshape.475), calls=%async_computation.4 | async-start | bytes 131072 | tf_op jit(solution)/shard_map/all_to_all | solution.py:174
  242.4 11.7 %all-to-all-start.6 = ((f32[3,8,512]{2,0,1:T(4,128)}), f32[3,8,512]{2,0,1:T(4,128)S(1)}, u32[]{:S(2)}, u32[]{:S(2)}) async-start(f32[3,8,512]{2,0,1:T(4,128)} %reshape.476), calls=%async_computation.6 | async-start | bytes 131072 | tf_op jit(solution)/shard_map/all_to_all | solution.py:181
  285.6 29.9 %all-to-all-start.7 = ((f32[8,1,1536]{2,1,0:T(1,128)}), f32[8,1,1536]{2,1,0:T(1,128)S(1)}, u32[]{:S(2)}, u32[]{:S(2)}) async-start(f32[8,1,1536]{2,1,0:T(1,128)} %reshape.496), calls=%async_computation.7 | async-start | bytes 98304 | tf_op jit(solution)/shard_map/all_to_all | solution.py:196
  289.0 257.3 %all-reduce.4.cloned.1.call-start = ((), (), s32[]{:S(2)}) async-start(), calls=%async_computation.14 | async-start | bytes 393216 | tf_op jit(solution)/shard_map/psum | solution.py:302
  315.5 20.2 %all-to-all-start.9 = ((f32[8,1,1536]{2,1,0:T(1,128)}), f32[8,1,1536]{2,1,0:T(1,128)S(1)}, u32[]{:S(2)}, u32[]{:S(2)}) async-start(f32[8,1,1536]{2,1,0:T(1,128)} %reshape.500), calls=%async_computation.9 | async-start | bytes 98304 | tf_op jit(solution)/shard_map/all_to_all | solution.py:203
  335.7 98.6 %all-to-all-start.8 = ((f32[32,1,384]{2,1,0:T(1,128)}), f32[32,1,384]{2,1,0:T(1,128)S(1)}, u32[]{:S(2)}, u32[]{:S(2)}) async-start(f32[32,1,384]{2,1,0:T(1,128)} %reshape.498), calls=%async_computation.8 | async-start | bytes 98304 | tf_op jit(solution)/shard_map/all_to_all | solution.py:212
  434.2 12.0 %all-to-all-start.10 = ((f32[32,1,384]{2,1,0:T(1,128)}), f32[32,1,384]{2,1,0:T(1,128)S(1)}, u32[]{:S(2)}, u32[]{:S(2)}) async-start(f32[32,1,384]{2,1,0:T(1,128)} %reshape.502), calls=%async_computation.10 | async-start | bytes 98304 | tf_op jit(solution)/shard_map/all_to_all | solution.py:219
  451.9 12.1 %all-to-all-start.12 = ((f32[32,1,384]{2,1,0:T(1,128)}), f32[32,1,384]{2,1,0:T(1,128)S(1)}, u32[]{:S(2)}, u32[]{:S(2)}) async-start(f32[32,1,384]{2,1,0:T(1,128)} %reshape.506), calls=%async_computation.12 | async-start | bytes 98304 | tf_op jit(solution)/shard_map/all_to_all | solution.py:233
  464.0 11.3 %all-to-all-start.11 = ((f32[32,1,384]{2,1,0:T(1,128)}), f32[32,1,384]{2,1,0:T(1,128)S(1)}, u32[]{:S(2)}, u32[]{:S(2)}) async-start(f32[32,1,384]{2,1,0:T(1,128)} %reshape.504), calls=%async_computation.11 | async-start | bytes 98304 | tf_op jit(solution)/shard_map/all_to_all | solution.py:232
  477.7 70.2 %all-to-all-start.13 = ((f32[3,8,512]{2,0,1:T(4,128)}), f32[3,8,512]{2,0,1:T(4,128)S(1)}, u32[]{:S(2)}, u32[]{:S(2)}) async-start(f32[3,8,512]{2,0,1:T(4,128)} %copy.204), calls=%async_computation.13 | async-start | bytes 131072 | tf_op jit(solution)/shard_map/all_to_all | solution.py:241
  (43 other events, 436.5 us)
Sparse Core Ops, SparseCore 0:
  296.0 250.2 all-reduce.3
where the time goes:
time: 566 us; the launch traced here: 556 us
  starting transfers between devices  114 us (20%)
  waiting for transfers between devices  109 us (19%)
  other arithmetic  97.2 us (17%)
  local copies, waits for them, and re-layouts  90 us (16%)
  blocking collectives  79.2 us (14%)
  matrix products  40.8 us (7%)
  between operations  25.4 us (4%)
    psum x1, blocking collectives, local(): lax.psum((jnp.stack(grads_now), jnp.stack(grads_past), jnp.stack(grads_mi...  79.2 us
    unnamed x8, other arithmetic  76 us
    psum x1, waiting for transfers between devices, local(): lax.psum((jnp.stack(grads_now), jnp.stack(grads_past), jnp.stack(grads_mi...  63.4 us
    unnamed x117, local copies, waits for them, and re-layouts  39.2 us
    all_to_all x1, starting transfers between devices, per_axis_filter(): lax.all_to_all(signal.reshape(3, 1, segment), 'rows', split_axis=2, conca...  21 us
    ppermute x6, starting transfers between devices, from_behind(): return lax.ppermute(array, axis, pairs)  16.5 us
    all_to_all x1, starting transfers between devices, per_axis_filter(): lax.all_to_all(signals[0].reshape(signal_count, rows_count, 1, piece_len)...  14.5 us
    gather x2, local copies, waits for them, and re-layouts, local_section(): weights = jnp.take(psd_weight, bins_here, axis=1)  11.5 us
  transfers between devices with their start and end apart: 21, of which 15 were waited for; matrix products, arithmetic and copies ran while one was open for 23% of the time, Pallas kernels for 0%

commit v1 on v0

--- a/solution.py
+++ b/solution.py
@@ -5,6 +5,10 @@
 from jax.sharding import PartitionSpec as P
 
 DMAX = 256
+
+
+def use_patch_by_axis(x0):
+    return jax.lax.psum(jax.lax.psum(x0, "cols"), "rows")
 
 
 def from_behind(array, axis, by):
@@ -299,9 +303,8 @@
         )
     input_grad = jnp.dot(lift_weight.T, grad_field, precision=lax.Precision.HIGHEST)
     lift_part = jnp.dot(grad_field, whitened.T, precision=lax.Precision.HIGHEST)
-    summed = lax.psum(
-        (jnp.stack(grads_now), jnp.stack(grads_past), jnp.stack(grads_mix), lift_part),
-        ("rows", "cols"),
+    summed = use_patch_by_axis(
+        (jnp.stack(grads_now), jnp.stack(grads_past), jnp.stack(grads_mix), lift_part)
     )
     scaling = 1.0 / math.sqrt(float(segment * lax.axis_size("rows") * lax.axis_size("cols")))
     data_grad = per_axis_filter(input_grad, psd_bin, psd_weight)

time: 566 us -> 634 us (1.12)
  the two profiles are of different devices: /device:TPU:1 before, /device:TPU:2 now
where the time goes in v1:
time: 634 us; the launch traced here: 624 us
  blocking collectives  152 us (24%)
  starting transfers between devices  121 us (19%)
  waiting for transfers between devices  106 us (17%)
  other arithmetic  95.4 us (15%)
  local copies, waits for them, and re-layouts  86.5 us (14%)
  matrix products  37.7 us (6%)
  between operations  25.2 us (4%)
    psum x2, blocking collectives, use_patch_by_axis(): return jax.lax.psum(jax.lax.psum(x0, 'cols'), 'rows')  152 us
    unnamed x8, other arithmetic  74.8 us
    psum x2, waiting for transfers between devices, use_patch_by_axis(): return jax.lax.psum(jax.lax.psum(x0, 'cols'), 'rows')  61.7 us
    unnamed x101, local copies, waits for them, and re-layouts  39.1 us
    all_to_all x1, starting transfers between devices, per_axis_filter(): lax.all_to_all(signals[0].reshape(signal_count, rows_count, 1, piece_len)...  18.4 us
    all_to_all x1, starting transfers between devices, per_axis_filter(): lax.all_to_all(signal.reshape(3, 1, segment), 'rows', split_axis=2, conca...  17.7 us
    ppermute x6, starting transfers between devices, from_behind(): return lax.ppermute(array, axis, pairs)  16.8 us
  transfers between devices with their start and end apart: 22, of which 15 were waited for; matrix products, arithmetic and copies ran while one was open for 24% of the time, Pallas kernels for 0%

profile of v1, /device:TPU:2, one launch (start us, length us, event | category | flops | bytes accessed | tf_op | source)
XLA Modules:
  0.0 624.0 jit_solution(14151084490687440475)
XLA Ops:
  19.9 10.8 %gather_fusion = f32[4096,2]{1,0:T(8,128)S(1)} fusion(f32[2,1024]{0,1:T(8,128)S(1)} %copy.178, s32[4096]{0:T(1024)S(1)} %broadcast_clamp_fusion), kind=kCustom, calls=%fused_computation | custom fusion | bytes 81920 | tf_op jit(solution)/shard_map/jit(_take)/gather | solution.py:114
  87.3 20.4 %reduce.4 = f32[4096,3]{1,0:T(8,128)} reduce(f32[4096,1,3]{2,1,0:T(1,128)} %bitcast.335, f32[]{:T(128)} %broadcast.734), dimensions={1}, to_apply=%bitcast.265.reduce_sub_computation | reduce | bytes 98308
  111.5 17.7 %all-to-all-start = ((f32[8,1,1536]{2,1,0:T(1,128)}), f32[8,1,1536]{2,1,0:T(1,128)S(1)}, u32[]{:S(2)}, u32[]{:S(2)}) async-start(f32[8,1,1536]{2,1,0:T(1,128)} %reshape.486), calls=%async_computation | async-start | bytes 98304 | tf_op jit(solution)/shard_map/all_to_all | solution.py:142
  131.4 6.0 all-to-all-done
  138.2 4.4 reshape.487
  154.6 18.4 %all-to-all-start.1 = ((f32[32,1,384]{2,1,0:T(1,128)}), f32[32,1,384]{2,1,0:T(1,128)S(1)}, u32[]{:S(2)}, u32[]{:S(2)}) async-start(f32[32,1,384]{2,1,0:T(1,128)} %reshape.488), calls=%async_computation.1 | async-start | bytes 98304 | tf_op jit(solution)/shard_map/all_to_all | solution.py:150
  179.3 7.9 %all-to-all-start.2 = ((f32[32,1,384]{2,1,0:T(1,128)}), f32[32,1,384]{2,1,0:T(1,128)S(1)}, u32[]{:S(2)}, u32[]{:S(2)}) async-start(f32[32,1,384]{2,1,0:T(1,128)} %reshape.490), calls=%async_computation.2 | async-start | bytes 98304 | tf_op jit(solution)/shard_map/all_to_all | solution.py:157
  201.5 5.9 all-to-all-start.3
  213.7 4.9 all-to-all-start.5
  231.1 5.6 all-to-all-done.4
  241.0 7.4 %all-to-all-done.6 = f32[3,8,512]{2,0,1:T(4,128)S(1)} async-done(((f32[3,8,512]{2,0,1:T(4,128)}), f32[3,8,512]{2,0,1:T(4,128)S(1)}, u32[]{:S(2)}, u32[]{:S(2)}) %all-to-all-start.6) | async-done | bytes 49184 | tf_op jit(solution)/shard_map/all_to_all | solution.py:185
  256.9 19.4 %reduce.12 = f32[4096,3]{1,0:T(8,128)} reduce(f32[4096,1,3]{2,1,0:T(1,128)S(1)} %bitcast.337, f32[]{:T(128)} %broadcast.734), dimensions={1}, to_apply=%bitcast.275.reduce_sub_computation | reduce | bytes 98308
  286.1 19.4 %reduce.16 = f32[4096,3]{1,0:T(8,128)} reduce(f32[4096,1,3]{2,1,0:T(1,128)S(1)} %bitcast.338, f32[]{:T(128)} %broadcast.734), dimensions={1}, to_apply=%bitcast.279.reduce_sub_computation | reduce | bytes 98308
  309.3 7.2 %all-to-all-start.9 = ((f32[8,1,1536]{2,1,0:T(1,128)}), f32[8,1,1536]{2,1,0:T(1,128)S(1)}, u32[]{:S(2)}, u32[]{:S(2)}) async-start(f32[8,1,1536]{2,1,0:T(1,128)} %reshape.500), calls=%async_computation.9 | async-start | bytes 98304 | tf_op jit(solution)/shard_map/all_to_all | solution.py:207
  317.4 120.0 %all-reduce = (f32[3,64,64]{2,1,0:T(8,128)S(1)}, f32[64,3]{0,1:T(4,128)S(1)}) all-reduce(f32[3,64,64]{2,1,0:T(8,128)S(1)} %pad_maximum_fusion.6, f32[64,3]{0,1:T(4,128)S(1)} %fusion.359), channel_id=1, replica_groups=mesh['rows'=8,'cols'=32] {'cols'}, use_global_device_ids=true, to_apply=%region_4.0 | all-reduce | flops 12480 | bytes 99840 | tf_op jit(solution)/shard_map/psum | solution.py:11
  449.7 9.1 %all-to-all-start.8 = ((f32[32,1,384]{2,1,0:T(1,128)}), f32[32,1,384]{2,1,0:T(1,128)S(1)}, u32[]{:S(2)}, u32[]{:S(2)}) async-start(f32[32,1,384]{2,1,0:T(1,128)} %reshape.498), calls=%async_computation.8 | async-start | bytes 98304 | tf_op jit(solution)/shard_map/all_to_all | solution.py:216
  458.8 32.0 %all-reduce.2 = (f32[3,64,64]{2,1,0:T(8,128)S(1)}, f32[64,3]{0,1:T(4,128)S(1)}) all-reduce(f32[3,64,64]{2,1,0:T(8,128)S(1)} %get-tuple-element.5, f32[64,3]{0,1:T(4,128)S(1)} %get-tuple-element.6), channel_id=1, replica_groups=mesh['rows'=8,'cols'=32] {'rows'}, use_global_device_ids=true, to_apply=%region_5.0 | all-reduce | flops 12480 | bytes 99840 | tf_op jit(solution)/shard_map/psum | solution.py:11
  503.2 7.8 %all-to-all-start.10 = ((f32[32,1,384]{2,1,0:T(1,128)}), f32[32,1,384]{2,1,0:T(1,128)S(1)}, u32[]{:S(2)}, u32[]{:S(2)}) async-start(f32[32,1,384]{2,1,0:T(1,128)} %reshape.502), calls=%async_computation.10 | async-start | bytes 98304 | tf_op jit(solution)/shard_map/all_to_all | solution.py:223
  522.8 5.9 all-to-all-start.12
  530.4 4.6 all-to-all-done.12
  535.0 4.9 all-to-all-start.11
  542.0 4.3 all-to-all-done.11
  548.7 4.4 all-to-all-start.13
  553.1 61.7 %all-reduce.9.cloned.1.call-done = (f32[3,128,64]{1,2,0:T(8,128)}, f32[3,128,64]{1,2,0:T(8,128)}) async-done(((f32[3,128,64]{1,2,0:T(8,128)}, f32[3,128,64]{1,2,0:T(8,128)}), (f32[3,128,64]{1,2,0:T(8,128)}, f32[3,128,64]{1,2,0:T(8,128)})) %all-reduce.9.cloned.1.call-update) | async-done | bytes 196624 | tf_op jit(solution)/shard_map/psum | solution.py:11
  (279 shorter events, 188.7 us)
Async XLA Ops:
  9.2 34.7 %copy-start = (bf16[64,4096]{1,0:T(8,128)(2,1)}, bf16[64,4096]{1,0:T(8,128)(2,1)S(1)}, u32[]{:S(2)}) copy-start(bf16[64,4096]{1,0:T(8,128)(2,1)S(1)} %fusion.33) | copy-start | bytes 1572868
  9.9 34.1 %collective-permute-start = (bf16[64,256]{1,0:T(8,128)(2,1)}, bf16[64,256]{1,0:T(8,128)(2,1)}, u32[]{:S(2)}, u32[]{:S(2)}) collective-permute-start(bf16[64,256]{1,0:T(8,128)(2,1)} %slice.140), channel_id=1, source_target_pairs={{0,1},{1,2},{2,3},{3,4},{4,5},{5,6},{6,7},{7,8},{8,9},{9,10},{10,1... | collective-permute-start | bytes 98312 | tf_op jit(solution)/shard_map/ppermute | solution.py:17
  46.5 5.2 collective-permute-start.1
  53.0 5.2 collective-permute-start.2
  62.2 3.8 collective-permute-start.3
  68.8 5.6 collective-permute-start.4
  75.8 53.4 %copy-start.2 = (bf16[64,4096]{1,0:T(8,128)(2,1)}, bf16[64,4096]{1,0:T(8,128)(2,1)S(1)}, u32[]{:S(2)}) copy-start(bf16[64,4096]{1,0:T(8,128)(2,1)S(1)} %get-tuple-element.13) | copy-start | bytes 1572868
  76.1 5.6 collective-permute-start.5
  111.5 25.8 %all-to-all-start = ((f32[8,1,1536]{2,1,0:T(1,128)}), f32[8,1,1536]{2,1,0:T(1,128)S(1)}, u32[]{:S(2)}, u32[]{:S(2)}) async-start(f32[8,1,1536]{2,1,0:T(1,128)} %reshape.486), calls=%async_computation | async-start | bytes 98304 | tf_op jit(solution)/shard_map/all_to_all | solution.py:142
  154.6 24.7 %all-to-all-start.1 = ((f32[32,1,384]{2,1,0:T(1,128)}), f32[32,1,384]{2,1,0:T(1,128)S(1)}, u32[]{:S(2)}, u32[]{:S(2)}) async-start(f32[32,1,384]{2,1,0:T(1,128)} %reshape.488), calls=%async_computation.1 | async-start | bytes 98304 | tf_op jit(solution)/shard_map/all_to_all | solution.py:150
  179.3 14.1 %all-to-all-start.2 = ((f32[32,1,384]{2,1,0:T(1,128)}), f32[32,1,384]{2,1,0:T(1,128)S(1)}, u32[]{:S(2)}, u32[]{:S(2)}) async-start(f32[32,1,384]{2,1,0:T(1,128)} %reshape.490), calls=%async_computation.2 | async-start | bytes 98304 | tf_op jit(solution)/shard_map/all_to_all | solution.py:157
  201.5 12.2 %all-to-all-start.3 = ((f32[32,1,384]{2,1,0:T(1,128)}), f32[32,1,384]{2,1,0:T(1,128)S(1)}, u32[]{:S(2)}, u32[]{:S(2)}) async-start(f32[32,1,384]{2,1,0:T(1,128)} %reshape.492), calls=%async_computation.3 | async-start | bytes 98304 | tf_op jit(solution)/shard_map/all_to_all | solution.py:174
  213.7 11.3 %all-to-all-start.5 = ((f32[32,1,384]{2,1,0:T(1,128)}), f32[32,1,384]{2,1,0:T(1,128)S(1)}, u32[]{:S(2)}, u32[]{:S(2)}) async-start(f32[32,1,384]{2,1,0:T(1,128)} %reshape.494), calls=%async_computation.5 | async-start | bytes 98304 | tf_op jit(solution)/shard_map/all_to_all | solution.py:175
  225.0 11.7 %all-to-all-start.4 = ((f32[3,8,512]{2,0,1:T(4,128)}), f32[3,8,512]{2,0,1:T(4,128)S(1)}, u32[]{:S(2)}, u32[]{:S(2)}) async-start(f32[3,8,512]{2,0,1:T(4,128)} %reshape.475), calls=%async_computation.4 | async-start | bytes 131072 | tf_op jit(solution)/shard_map/all_to_all | solution.py:178
  228.3 312.2 %all-reduce.7.cloned.1.call-start = ((), (), s32[]{:S(2)}) async-start(), calls=%async_computation.14 | async-start | bytes 393216 | tf_op jit(solution)/shard_map/psum | solution.py:11
  236.6 11.8 %all-to-all-start.6 = ((f32[3,8,512]{2,0,1:T(4,128)}), f32[3,8,512]{2,0,1:T(4,128)S(1)}, u32[]{:S(2)}, u32[]{:S(2)}) async-start(f32[3,8,512]{2,0,1:T(4,128)} %reshape.476), calls=%async_computation.6 | async-start | bytes 131072 | tf_op jit(solution)/shard_map/all_to_all | solution.py:185
  280.1 29.2 %all-to-all-start.7 = ((f32[8,1,1536]{2,1,0:T(1,128)}), f32[8,1,1536]{2,1,0:T(1,128)S(1)}, u32[]{:S(2)}, u32[]{:S(2)}) async-start(f32[8,1,1536]{2,1,0:T(1,128)} %reshape.496), calls=%async_computation.7 | async-start | bytes 98304 | tf_op jit(solution)/shard_map/all_to_all | solution.py:200
  309.3 140.4 %all-to-all-start.9 = ((f32[8,1,1536]{2,1,0:T(1,128)}), f32[8,1,1536]{2,1,0:T(1,128)S(1)}, u32[]{:S(2)}, u32[]{:S(2)}) async-start(f32[8,1,1536]{2,1,0:T(1,128)} %reshape.500), calls=%async_computation.9 | async-start | bytes 98304 | tf_op jit(solution)/shard_map/all_to_all | solution.py:207
  449.7 53.5 %all-to-all-start.8 = ((f32[32,1,384]{2,1,0:T(1,128)}), f32[32,1,384]{2,1,0:T(1,128)S(1)}, u32[]{:S(2)}, u32[]{:S(2)}) async-start(f32[32,1,384]{2,1,0:T(1,128)} %reshape.498), calls=%async_computation.8 | async-start | bytes 98304 | tf_op jit(solution)/shard_map/all_to_all | solution.py:216
  503.2 13.9 %all-to-all-start.10 = ((f32[32,1,384]{2,1,0:T(1,128)}), f32[32,1,384]{2,1,0:T(1,128)S(1)}, u32[]{:S(2)}, u32[]{:S(2)}) async-start(f32[32,1,384]{2,1,0:T(1,128)} %reshape.502), calls=%async_computation.10 | async-start | bytes 98304 | tf_op jit(solution)/shard_map/all_to_all | solution.py:223
  522.8 12.2 %all-to-all-start.12 = ((f32[32,1,384]{2,1,0:T(1,128)}), f32[32,1,384]{2,1,0:T(1,128)S(1)}, u32[]{:S(2)}, u32[]{:S(2)}) async-start(f32[32,1,384]{2,1,0:T(1,128)} %reshape.506), calls=%async_computation.12 | async-start | bytes 98304 | tf_op jit(solution)/shard_map/all_to_all | solution.py:237
  535.0 11.3 %all-to-all-start.11 = ((f32[32,1,384]{2,1,0:T(1,128)}), f32[32,1,384]{2,1,0:T(1,128)S(1)}, u32[]{:S(2)}, u32[]{:S(2)}) async-start(f32[32,1,384]{2,1,0:T(1,128)} %reshape.504), calls=%async_computation.11 | async-start | bytes 98304 | tf_op jit(solution)/shard_map/all_to_all | solution.py:236
  540.0 74.8 %all-reduce.9.cloned.1.call-start = ((), (), s32[]{:S(2)}) async-start(), calls=%async_computation.15 | async-start | bytes 393216 | tf_op jit(solution)/shard_map/psum | solution.py:11
  548.7 67.6 %all-to-all-start.13 = ((f32[3,8,512]{2,0,1:T(4,128)}), f32[3,8,512]{2,0,1:T(4,128)S(1)}, u32[]{:S(2)}, u32[]{:S(2)}) async-start(f32[3,8,512]{2,0,1:T(4,128)} %copy.204), calls=%async_computation.13 | async-start | bytes 131072 | tf_op jit(solution)/shard_map/all_to_all | solution.py:245
  (36 other events, 349.4 us)
Sparse Core Ops, SparseCore 0:
  233.1 109.6 all-reduce.6
  543.1 71.5 all-reduce.8
